TPU v7x, 32 devices: a whole 2x2x4 slice. The times are simulated.
32 devices in a mesh: rep: 2 (over y), space: 4 (over z), tm: 4 (over x, core).
Axes of the slice: x: 2, y: 2, z: 4, core: 2. Of those that a mesh axis runs over, the one named last changes fastest.
Arguments:
- inputs: bfloat16 [16, 4, 96, 192], P(('rep', 'tm'), 'space'), parts along dimension 0, may hold values from -6 to 6
- cotangent: bfloat16 [16, 4, 96, 192], P(('rep', 'tm'), 'space'), parts along dimension 0, may hold values from -6 to 6
- weight: bfloat16 [3, 3, 3, 192, 192], replicated, may hold values from -0.078125 to 0.078125
Outputs:
- input_grad: bfloat16 [16, 4, 96, 192], P(('rep', 'tm'), 'space'), parts along dimension 0
- weight_grad: float32 [3, 3, 3, 384, 192], P(None, None, None, ('rep', 'tm'), 'space'), parts along dimension 3
There are 2 independent parts, one for each index of `rep`. A program takes and returns all parts, laid end to end along the dimension named above; an argument that names none is the same for every part. Nothing has to cross between parts.
All inputs are finite; a program needn't handle non-finite values.
Results may differ from a plain program's by a relative error of at most 0.0049.
Values may be sent and summed in bfloat16 or wider, within the bound.
A program may use at most 128 MiB of HBM per device.

v0:
```python
import math

import jax
import jax.numpy as jnp
from jax import lax
from jax.sharding import PartitionSpec as P


def passed_along(array, axis, by):
    length = lax.axis_size(axis)
    pairs = [(i, i + by) for i in range(length) if 0 <= i + by < length]
    return lax.ppermute(array, axis, pairs)


def extended_2(cells, sides, width):
    for axis, dim in sides:
        count = lax.axis_size(axis)
        ends = count - 1
        head = lax.slice_in_dim(cells, 0, width, axis=dim)
        tail = lax.slice_in_dim(cells, cells.shape[dim] - width, cells.shape[dim], axis=dim)
        cells = jnp.concatenate(
            [
                lax.ppermute(tail, axis, [(i, (i + 1) % count) for i in range(ends)]),
                cells,
                lax.ppermute(head, axis, [((i + 1) % count, i) for i in range(ends)]),
            ],
            axis=dim,
        )
    return cells


def local(inputs, cotangent, weight):
    frame_count, row_count, col_count, in_channels = inputs.shape
    out_channels = cotangent.shape[3]
    cell_count = frame_count * row_count * col_count
    space_size = lax.axis_size("space")
    time_size = lax.axis_size("tm")
    factor = 1.0 / math.sqrt(cell_count * space_size * time_size)
    earlier = passed_along(inputs, "tm", 1)
    extended = jnp.concatenate([earlier, inputs], axis=0)
    rimmed = extended_2(extended, (("space", 1),), 1)
    padded = jnp.pad(rimmed, ((0, 0), (0, 0), (1, 1), (0, 0)))
    outputs = jnp.zeros((cell_count, out_channels), jnp.float32)
    for depth_tap in range(3):
        for row_tap in range(3):
            for col_tap in range(3):
                window = padded[
                    depth_tap : depth_tap + frame_count,
                    row_tap : row_tap + row_count,
                    col_tap : col_tap + col_count,
                ].reshape(cell_count, in_channels)
                outputs = outputs + jnp.dot(
                    window, weight[depth_tap, row_tap, col_tap], preferred_element_type=jnp.float32
                )
    logistic = jax.nn.sigmoid(outputs)
    derivative = logistic * (1.0 + outputs * (1.0 - logistic))
    upstream = (
        cotangent.reshape(cell_count, out_channels).astype(jnp.float32) * derivative
    ).astype(jnp.bfloat16)
    upstream_grid = upstream.reshape(frame_count, row_count, col_count, out_channels)
    arriving = passed_along(upstream_grid, "tm", -1)
    following = jnp.concatenate([upstream_grid, arriving], axis=0)
    following = extended_2(following, (("space", 1),), 1)
    following = jnp.pad(following, ((0, 0), (0, 0), (1, 1), (0, 0)))
    input_grad = jnp.zeros((cell_count, in_channels), jnp.float32)
    tap_grads = []
    for depth_tap in range(3):
        for row_tap in range(3):
            for col_tap in range(3):
                returned = following[
                    2 - depth_tap : 2 - depth_tap + frame_count,
                    2 - row_tap : 2 - row_tap + row_count,
                    2 - col_tap : 2 - col_tap + col_count,
                ].reshape(cell_count, out_channels)
                input_grad = input_grad + lax.dot_general(
                    returned,
                    weight[depth_tap, row_tap, col_tap],
                    (((1,), (1,)), ((), ())),
                    preferred_element_type=jnp.float32,
                )
                window = padded[
                    depth_tap : depth_tap + frame_count,
                    row_tap : row_tap + row_count,
                    col_tap : col_tap + col_count,
                ].reshape(cell_count, in_channels)
                tap_grads.append(
                    lax.dot_general(
                        window,
                        upstream,
                        (((0,), (0,)), ((), ())),
                        preferred_element_type=jnp.float32,
                    )
                )
    partial_grad = jnp.stack(tap_grads) * factor
    in_share = in_channels // time_size
    out_share = out_channels // space_size
    blocks = partial_grad.reshape(27, in_channels, space_size, out_share)
    blocks = blocks.transpose(2, 0, 1, 3).reshape(space_size * 27, in_channels, out_share)
    spatial_sum = lax.psum_scatter(blocks, "space", scatter_dimension=0, tiled=True)
    blocks = spatial_sum.reshape(27, time_size, in_share, out_share)
    blocks = blocks.transpose(1, 0, 2, 3).reshape(time_size * 27, in_share, out_share)
    owned_part = lax.psum_scatter(blocks, "tm", scatter_dimension=0, tiled=True)
    input_grad = input_grad.reshape(frame_count, row_count, col_count, in_channels).astype(
        jnp.bfloat16
    )
    return (input_grad, owned_part.reshape(3, 3, 3, in_share, out_share))


def solution(mesh):
    placed = (P(("rep", "tm"), "space", None, None), P(("rep", "tm"), "space", None, None), P())
    return jax.shard_map(
        local,
        mesh=mesh,
        in_specs=placed,
        out_specs=(
            P(("rep", "tm"), "space", None, None),
            P(None, None, None, ("rep", "tm"), "space"),
        ),
        check_vma=False,
    )
```

profile of v0, /device:TPU:1, one launch (start us, length us, event | category | flops | bytes accessed | tf_op | source)
XLA Modules:
  0.0 195.3 jit_solution(14592667124595192674)
XLA Ops:
  7.2 4.6 %collective-permute-start = (bf16[2,1,96,192]{3,2,1,0:T(8,128)(2,1)}, bf16[2,1,96,192]{3,2,1,0:T(8,128)(2,1)S(1)}, u32[]{:S(2)}, u32[]{:S(2)}) collective-permute-start(bf16[2,1,96,192]{3,2,1,0:T(8,128)(2,1)} %param.3), channel_id=1, source_target_pairs={{0,1},{1,2},{2,3},{4,5},{5,6},{6,7},{8,9},{9,10},{10,11},{12,13},{... | collective-permute-start | bytes 221192 | tf_op jit(solution)/shard_map/ppermute | solution.py:12
  11.9 1.9 collective-permute-done
  14.7 3.2 %collective-permute-start.1 = (bf16[4,1,96,192]{3,2,1,0:T(8,128)(2,1)S(1)}, bf16[4,1,96,192]{3,2,1,0:T(8,128)(2,1)S(1)}, u32[]{:S(2)}, u32[]{:S(2)}) collective-permute-start(bf16[4,1,96,192]{3,2,1,0:T(8,128)(2,1)S(1)} %constant_dynamic-update-slice_fusion), channel_id=1, source_target_pairs={{0,4},{4,8},{8,12},{1,5},{5,9},{9,13},{2,6},{6,10},{10,14},{3,7},{... | collective-permute-start | bytes 442376 | tf_op jit(solution)/shard_map/ppermute | solution.py:23
  17.9 1.3 collective-permute-start.2
  19.2 1.8 collective-permute-done.1
  21.0 4.1 %collective-permute-done.2 = bf16[4,1,96,192]{3,2,1,0:T(8,128)(2,1)S(1)} collective-permute-done((bf16[4,1,96,192]{3,2,1,0:T(8,128)(2,1)S(1)}, bf16[4,1,96,192]{3,2,1,0:T(8,128)(2,1)S(1)}, u32[]{:S(2)}, u32[]{:S(2)}) %collective-permute-start.2) | collective-permute-done | bytes 147488 | tf_op jit(solution)/shard_map/ppermute | solution.py:25
  32.8 1.1 fusion.38
  33.9 1.1 fusion.37
  35.0 1.1 fusion.36
  36.0 1.1 fusion.35
  38.1 1.1 fusion.34
  39.2 1.1 fusion.33
  44.6 2.7 %copy.35 = f32[4,27,192,48]{2,3,1,0:T(8,128)} copy(f32[4,27,192,48]{2,3,0,1:T(8,128)S(1)} %multiply_bitcast_fusion) | data formatting | bytes 7962624 | tf_op jit(solution)/shard_map/transpose | solution.py:98
  47.4 1.9 collective-permute-start.3
  49.3 5.2 %collective-permute-done.3 = bf16[2,1,96,192]{3,2,0,1:T(8,128)(2,1)S(1)} collective-permute-done((bf16[2,1,96,192]{3,2,0,1:T(8,128)(2,1)S(1)}, bf16[2,1,96,192]{3,2,0,1:T(8,128)(2,1)S(1)}, u32[]{:S(2)}, u32[]{:S(2)}) %collective-permute-start.3) | collective-permute-done | bytes 73760 | tf_op jit(solution)/shard_map/ppermute | solution.py:12
  54.6 3.2 %collective-permute-start.4 = (bf16[4,1,96,192]{3,2,0,1:T(8,128)(2,1)S(1)}, bf16[4,1,96,192]{3,2,0,1:T(8,128)(2,1)S(1)}, u32[]{:S(2)}, u32[]{:S(2)}) collective-permute-start(bf16[4,1,96,192]{3,2,0,1:T(8,128)(2,1)S(1)} %pad_maximum_fusion), channel_id=1, source_target_pairs={{0,4},{4,8},{8,12},{1,5},{5,9},{9,13},{2,6},{6,10},{10,14},{3,7},{... | collective-permute-start | bytes 442376 | tf_op jit(solution)/shard_map/ppermute | solution.py:23
  57.8 1.3 collective-permute-start.5
  59.1 6.3 %collective-permute-done.4 = bf16[4,1,96,192]{3,2,0,1:T(8,128)(2,1)S(1)} collective-permute-done((bf16[4,1,96,192]{3,2,0,1:T(8,128)(2,1)S(1)}, bf16[4,1,96,192]{3,2,0,1:T(8,128)(2,1)S(1)}, u32[]{:S(2)}, u32[]{:S(2)}) %collective-permute-start.4) | collective-permute-done | bytes 147488 | tf_op jit(solution)/shard_map/ppermute | solution.py:23
  65.4 9.9 %collective-permute-done.5 = bf16[4,1,96,192]{3,2,0,1:T(8,128)(2,1)S(1)} collective-permute-done((bf16[4,1,96,192]{3,2,0,1:T(8,128)(2,1)S(1)}, bf16[4,1,96,192]{3,2,0,1:T(8,128)(2,1)S(1)}, u32[]{:S(2)}, u32[]{:S(2)}) %collective-permute-start.5) | collective-permute-done | bytes 147488 | tf_op jit(solution)/shard_map/ppermute | solution.py:25
  81.6 66.3 %reduce-scatter.3.cloned.1.call-done = f32[27,192,48]{1,2,0:T(8,128)} async-done(((f32[108,192,48]{1,2,0:T(8,128)}), f32[27,192,48]{1,2,0:T(8,128)}) %reduce-scatter.3.cloned.1.call-update) | async-done | bytes 995344 | tf_op jit(solution)/shard_map/reduce_scatter | solution.py:99
  147.9 2.6 %reshape.459 = f32[27,4,48,48]{2,1,3,0:T(4,128)S(1)} reshape(f32[27,192,48]{1,2,0:T(8,128)} %reduce-scatter.3.cloned.1.call-done) | data formatting | bytes 1990656 | tf_op jit(solution)/shard_map/reshape | solution.py:100
  150.5 2.6 %copy.36 = f32[4,27,48,48]{3,2,1,0:T(8,128)} copy(f32[4,27,48,48]{2,0,3,1:T(4,128)S(1)} %bitcast.495) | data formatting | bytes 1990656 | tf_op jit(solution)/shard_map/transpose | solution.py:101
  154.0 1.1 fusion.50
  155.1 1.1 fusion.4
  156.2 1.1 convolution_add_fusion.6
  157.3 1.1 fusion.3
  158.4 1.1 convolution_add_fusion.4
  159.5 1.1 convolution_add_fusion.3
  160.6 1.1 convolution_add_fusion.2
  161.7 1.1 convolution_add_fusion.1
  162.9 1.7 fusion.39
  164.6 23.8 %reduce-scatter.5.cloned.1.call-done = f32[27,48,48]{2,1,0:T(8,128)} async-done(((f32[108,48,48]{2,1,0:T(8,128)}), f32[27,48,48]{2,1,0:T(8,128)}) %reduce-scatter.5.cloned.1.call-update) | async-done | bytes 248848 | tf_op jit(solution)/shard_map/reduce_scatter | solution.py:102
  (169 shorter events, 20.4 us)
Async XLA Ops:
  7.2 18.5 %copy-start = (bf16[3,3,3,192,192]{4,3,2,1,0:T(8,128)(2,1)S(1)}, bf16[3,3,3,192,192]{4,3,2,1,0:T(8,128)(2,1)}, u32[]{:S(2)}) copy-start(bf16[3,3,3,192,192]{4,3,2,1,0:T(8,128)(2,1)} %param.5) | copy-start | bytes 5971972
  7.2 140.7 %reduce-scatter.3.cloned.1.call-start = ((), (), s32[]{:S(2)}) async-start(), calls=%async_computation.2 | async-start | bytes 6635520 | tf_op jit(solution)/shard_map/reduce_scatter | solution.py:99
  7.2 6.6 %collective-permute-start = (bf16[2,1,96,192]{3,2,1,0:T(8,128)(2,1)}, bf16[2,1,96,192]{3,2,1,0:T(8,128)(2,1)S(1)}, u32[]{:S(2)}, u32[]{:S(2)}) collective-permute-start(bf16[2,1,96,192]{3,2,1,0:T(8,128)(2,1)} %param.3), channel_id=1, source_target_pairs={{0,1},{1,2},{2,3},{4,5},{5,6},{6,7},{8,9},{9,10},{10,11},{12,13},{... | collective-permute-start | bytes 221192 | tf_op jit(solution)/shard_map/ppermute | solution.py:12
  14.7 6.3 %collective-permute-start.1 = (bf16[4,1,96,192]{3,2,1,0:T(8,128)(2,1)S(1)}, bf16[4,1,96,192]{3,2,1,0:T(8,128)(2,1)S(1)}, u32[]{:S(2)}, u32[]{:S(2)}) collective-permute-start(bf16[4,1,96,192]{3,2,1,0:T(8,128)(2,1)S(1)} %constant_dynamic-update-slice_fusion), channel_id=1, source_target_pairs={{0,4},{4,8},{8,12},{1,5},{5,9},{9,13},{2,6},{6,10},{10,14},{3,7},{... | collective-permute-start | bytes 442376 | tf_op jit(solution)/shard_map/ppermute | solution.py:23
  17.9 7.2 %collective-permute-start.2 = (bf16[4,1,96,192]{3,2,1,0:T(8,128)(2,1)S(1)}, bf16[4,1,96,192]{3,2,1,0:T(8,128)(2,1)S(1)}, u32[]{:S(2)}, u32[]{:S(2)}) collective-permute-start(bf16[4,1,96,192]{3,2,1,0:T(8,128)(2,1)S(1)} %constant_dynamic-update-slice_fusion), channel_id=1, source_target_pairs={{4,0},{8,4},{12,8},{5,1},{9,5},{13,9},{6,2},{10,6},{14,10},{7,3},{... | collective-permute-start | bytes 442376 | tf_op jit(solution)/shard_map/ppermute | solution.py:25
  19.2 9.5 %copy-start.28 = (bf16[2,1,96,192]{3,2,1,0:T(8,128)(2,1)}, bf16[2,1,96,192]{3,2,1,0:T(8,128)(2,1)S(1)}, u32[]{:S(2)}) copy-start(bf16[2,1,96,192]{3,2,1,0:T(8,128)(2,1)S(1)} %slice.414) | copy-start | bytes 221188
  25.5 2.1 %copy-start.4 = (bf16[2,1,96,192]{3,2,1,0:T(8,128)(2,1)}, bf16[2,1,96,192]{3,2,1,0:T(8,128)(2,1)S(1)}, u32[]{:S(2)}) copy-start(bf16[2,1,96,192]{3,2,1,0:T(8,128)(2,1)S(1)} %get-tuple-element.40) | copy-start | bytes 221188
  25.6 2.5 %copy-start.1 = (bf16[2,1,96,192]{3,2,1,0:T(8,128)(2,1)}, bf16[2,1,96,192]{3,2,1,0:T(8,128)(2,1)S(1)}, u32[]{:S(2)}) copy-start(bf16[2,1,96,192]{3,2,1,0:T(8,128)(2,1)S(1)} %get-tuple-element.36) | copy-start | bytes 221188
  26.9 2.7 %copy-start.18 = (bf16[2,1,96,192]{3,2,1,0:T(8,128)(2,1)}, bf16[2,1,96,192]{3,2,1,0:T(8,128)(2,1)S(1)}, u32[]{:S(2)}) copy-start(bf16[2,1,96,192]{3,2,1,0:T(8,128)(2,1)S(1)} %get-tuple-element.53) | copy-start | bytes 221188
  28.0 2.6 %copy-start.37 = (bf16[2,1,96,192]{3,2,1,0:T(8,128)(2,1)}, bf16[2,1,96,192]{3,2,1,0:T(8,128)(2,1)S(1)}, u32[]{:S(2)}) copy-start(bf16[2,1,96,192]{3,2,1,0:T(8,128)(2,1)S(1)} %get-tuple-element.50) | copy-start | bytes 221188
  32.7 7.6 %copy-start.25 = (bf16[2,1,96,192]{3,2,1,0:T(8,128)(2,1)S(1)}, bf16[2,1,96,192]{3,2,1,0:T(8,128)(2,1)}, u32[]{:S(2)}) copy-start(bf16[2,1,96,192]{3,2,1,0:T(8,128)(2,1)} %copy-done.24) | copy-start | bytes 221188
  32.7 7.8 %copy-start.15 = (bf16[2,1,96,192]{3,2,1,0:T(8,128)(2,1)S(1)}, bf16[2,1,96,192]{3,2,1,0:T(8,128)(2,1)}, u32[]{:S(2)}) copy-start(bf16[2,1,96,192]{3,2,1,0:T(8,128)(2,1)} %copy-done.14) | copy-start | bytes 221188
  32.7 8.0 %copy-start.2 = (bf16[2,1,96,192]{3,2,1,0:T(8,128)(2,1)S(1)}, bf16[2,1,96,192]{3,2,1,0:T(8,128)(2,1)}, u32[]{:S(2)}) copy-start(bf16[2,1,96,192]{3,2,1,0:T(8,128)(2,1)} %copy-done.1) | copy-start | bytes 221188
  32.7 8.1 %copy-start.23 = (bf16[2,1,96,192]{3,2,1,0:T(8,128)(2,1)S(1)}, bf16[2,1,96,192]{3,2,1,0:T(8,128)(2,1)}, u32[]{:S(2)}) copy-start(bf16[2,1,96,192]{3,2,1,0:T(8,128)(2,1)} %copy-done.22) | copy-start | bytes 221188
  32.7 8.3 %copy-start.13 = (bf16[2,1,96,192]{3,2,1,0:T(8,128)(2,1)S(1)}, bf16[2,1,96,192]{3,2,1,0:T(8,128)(2,1)}, u32[]{:S(2)}) copy-start(bf16[2,1,96,192]{3,2,1,0:T(8,128)(2,1)} %copy-done.12) | copy-start | bytes 221188
  32.7 8.6 %copy-start.29 = (bf16[2,1,96,192]{3,2,1,0:T(8,128)(2,1)S(1)}, bf16[2,1,96,192]{3,2,1,0:T(8,128)(2,1)}, u32[]{:S(2)}) copy-start(bf16[2,1,96,192]{3,2,1,0:T(8,128)(2,1)} %copy-done.28) | copy-start | bytes 221188
  36.0 5.9 %copy-start.21 = (bf16[2,1,96,192]{3,2,1,0:T(8,128)(2,1)S(1)}, bf16[2,1,96,192]{3,2,1,0:T(8,128)(2,1)}, u32[]{:S(2)}) copy-start(bf16[2,1,96,192]{3,2,1,0:T(8,128)(2,1)} %copy-done.20) | copy-start | bytes 221188
  37.1 5.0 %copy-start.11 = (bf16[2,1,96,192]{3,2,1,0:T(8,128)(2,1)S(1)}, bf16[2,1,96,192]{3,2,1,0:T(8,128)(2,1)}, u32[]{:S(2)}) copy-start(bf16[2,1,96,192]{3,2,1,0:T(8,128)(2,1)} %copy-done.10) | copy-start | bytes 221188
  39.2 3.3 %copy-start.19 = (bf16[2,1,96,192]{3,2,1,0:T(8,128)(2,1)S(1)}, bf16[2,1,96,192]{3,2,1,0:T(8,128)(2,1)}, u32[]{:S(2)}) copy-start(bf16[2,1,96,192]{3,2,1,0:T(8,128)(2,1)} %copy-done.18) | copy-start | bytes 221188
  40.3 2.3 %copy-start.9 = (bf16[2,1,96,192]{3,2,1,0:T(8,128)(2,1)S(1)}, bf16[2,1,96,192]{3,2,1,0:T(8,128)(2,1)}, u32[]{:S(2)}) copy-start(bf16[2,1,96,192]{3,2,1,0:T(8,128)(2,1)} %copy-done.8) | copy-start | bytes 221188
  40.7 2.3 %copy-start.30 = (f32[192,192]{1,0:T(8,128)S(1)}, f32[192,192]{1,0:T(8,128)}, u32[]{:S(2)}) copy-start(f32[192,192]{1,0:T(8,128)} %fusion.179) | copy-start | bytes 442372
  41.2 2.2 %copy-start.38 = (bf16[2,1,96,192]{3,2,1,0:T(8,128)(2,1)S(1)}, bf16[2,1,96,192]{3,2,1,0:T(8,128)(2,1)}, u32[]{:S(2)}) copy-start(bf16[2,1,96,192]{3,2,1,0:T(8,128)(2,1)} %copy-done.37) | copy-start | bytes 221188
  41.4 2.2 %copy-start.7 = (bf16[2,1,96,192]{3,2,1,0:T(8,128)(2,1)S(1)}, bf16[2,1,96,192]{3,2,1,0:T(8,128)(2,1)}, u32[]{:S(2)}) copy-start(bf16[2,1,96,192]{3,2,1,0:T(8,128)(2,1)} %copy-done.6) | copy-start | bytes 221188
  47.3 141.1 %reduce-scatter.5.cloned.1.call-start = ((), (), s32[]{:S(2)}) async-start(), calls=%async_computation.3 | async-start | bytes 3317760 | tf_op jit(solution)/shard_map/reduce_scatter | solution.py:102
  47.4 7.1 %collective-permute-start.3 = (bf16[2,1,96,192]{3,2,0,1:T(8,128)(2,1)S(1)}, bf16[2,1,96,192]{3,2,0,1:T(8,128)(2,1)S(1)}, u32[]{:S(2)}, u32[]{:S(2)}) collective-permute-start(bf16[2,1,96,192]{3,2,0,1:T(8,128)(2,1)S(1)} %bitcast.497), channel_id=1, source_target_pairs={{1,0},{2,1},{3,2},{5,4},{6,5},{7,6},{9,8},{10,9},{11,10},{13,12},{... | collective-permute-start | bytes 221192 | tf_op jit(solution)/shard_map/ppermute | solution.py:12
  54.6 10.8 %collective-permute-start.4 = (bf16[4,1,96,192]{3,2,0,1:T(8,128)(2,1)S(1)}, bf16[4,1,96,192]{3,2,0,1:T(8,128)(2,1)S(1)}, u32[]{:S(2)}, u32[]{:S(2)}) collective-permute-start(bf16[4,1,96,192]{3,2,0,1:T(8,128)(2,1)S(1)} %pad_maximum_fusion), channel_id=1, source_target_pairs={{0,4},{4,8},{8,12},{1,5},{5,9},{9,13},{2,6},{6,10},{10,14},{3,7},{... | collective-permute-start | bytes 442376 | tf_op jit(solution)/shard_map/ppermute | solution.py:23
  57.8 17.5 %collective-permute-start.5 = (bf16[4,1,96,192]{3,2,0,1:T(8,128)(2,1)S(1)}, bf16[4,1,96,192]{3,2,0,1:T(8,128)(2,1)S(1)}, u32[]{:S(2)}, u32[]{:S(2)}) collective-permute-start(bf16[4,1,96,192]{3,2,0,1:T(8,128)(2,1)S(1)} %pad_maximum_fusion), channel_id=1, source_target_pairs={{4,0},{8,4},{12,8},{5,1},{9,5},{13,9},{6,2},{10,6},{14,10},{7,3},{... | collective-permute-start | bytes 442376 | tf_op jit(solution)/shard_map/ppermute | solution.py:25
  153.1 3.1 %copy-start.33 = (bf16[2,1,96,192]{3,2,0,1:T(8,128)(2,1)S(1)}, bf16[2,1,96,192]{3,2,0,1:T(8,128)(2,1)}, u32[]{:S(2)}) copy-start(bf16[2,1,96,192]{3,2,0,1:T(8,128)(2,1)} %get-tuple-element.12) | copy-start | bytes 221188
  153.1 4.2 %copy-start.35 = (bf16[2,1,96,192]{3,2,0,1:T(8,128)(2,1)S(1)}, bf16[2,1,96,192]{3,2,0,1:T(8,128)(2,1)}, u32[]{:S(2)}) copy-start(bf16[2,1,96,192]{3,2,0,1:T(8,128)(2,1)} %get-tuple-element.47) | copy-start | bytes 221188
  153.1 5.3 %copy-start.32 = (bf16[2,1,96,192]{3,2,0,1:T(8,128)(2,1)S(1)}, bf16[2,1,96,192]{3,2,0,1:T(8,128)(2,1)}, u32[]{:S(2)}) copy-start(bf16[2,1,96,192]{3,2,0,1:T(8,128)(2,1)} %get-tuple-element.10) | copy-start | bytes 221188
  153.1 7.5 %copy-start.31 = (bf16[2,1,96,192]{3,2,0,1:T(8,128)(2,1)S(1)}, bf16[2,1,96,192]{3,2,0,1:T(8,128)(2,1)}, u32[]{:S(2)}) copy-start(bf16[2,1,96,192]{3,2,0,1:T(8,128)(2,1)} %get-tuple-element.9) | copy-start | bytes 221188
  153.1 9.7 %copy-start.39 = (bf16[2,1,96,192]{3,2,0,1:T(8,128)(2,1)S(1)}, bf16[2,1,96,192]{3,2,0,1:T(8,128)(2,1)}, u32[]{:S(2)}) copy-start(bf16[2,1,96,192]{3,2,0,1:T(8,128)(2,1)} %get-tuple-element.44) | copy-start | bytes 221188
  (17 other events, 31.1 us)
Sparse Core Ops, SparseCore 0:
  47.5 100.3 reduce-scatter.2
  153.3 35.1 reduce-scatter.4
where the time goes:
time: 197 us; the launch traced here: 195 us
  waiting for transfers between devices  119 us (60%)
  matrix products  30.4 us (15%)
  starting transfers between devices  15.6 us (8%)
  between operations  15 us (8%)
  local copies, waits for them, and re-layouts  13.5 us (7%)
    reduce_scatter x1, waiting for transfers between devices, local(): lax.psum_scatter(blocks, 'space', scatter_dimension=0, tiled=True)  66.3 us
    reduce_scatter x1, waiting for transfers between devices, local(): owned_part = lax.psum_scatter(blocks, 'tm', scatter_dimension=0, tiled=True)  23.8 us
    dot_general x27, matrix products, local(): lax.dot_general(returned, weight[depth_tap, row_tap, col_tap], (((1,), (1...  14.2 us
    ppermute x2, waiting for transfers between devices, extended_2(): lax.ppermute(head, axis, [((i + 1) % count, i) for i in range(ends)])  14.1 us
    dot_general x27, matrix products, local(): lax.dot_general(window, upstream, (((0,), (0,)), ((), ())), preferred_ele...  11.5 us
    ppermute x2, waiting for transfers between devices, extended_2(): lax.ppermute(tail, axis, [(i, (i + 1) % count) for i in range(ends)])  8.04 us
    ppermute x2, waiting for transfers between devices, passed_along(): return lax.ppermute(array, axis, pairs)  7.15 us
    ppermute x2, starting transfers between devices, passed_along(): return lax.ppermute(array, axis, pairs)  6.55 us
  transfers between devices with their start and end apart: 8, of which 8 were waited for; matrix products, arithmetic and copies ran while one was open for 9% of the time, Pallas kernels for 0%

commit v1 on v0

--- a/solution.py
+++ b/solution.py
@@ -1,9 +1,15 @@
+import functools
 import math
 
 import jax
 import jax.numpy as jnp
 from jax import lax
+from jax.experimental import pallas as pl
+from jax.experimental.pallas import tpu as pltpu
 from jax.sharding import PartitionSpec as P
+
+MESH = pl.DeviceIdType.MESH
+LANES = 128
 
 
 def passed_along(array, axis, by):
@@ -29,7 +35,7 @@
     return cells
 
 
-def local(inputs, cotangent, weight):
+def reduced(inputs, cotangent, weight):
     frame_count, row_count, col_count, in_channels = inputs.shape
     out_channels = cotangent.shape[3]
     cell_count = frame_count * row_count * col_count
@@ -106,10 +112,327 @@
     return (input_grad, owned_part.reshape(3, 3, 3, in_share, out_share))
 
 
+def shifted_rows(values, by, width):
+    count = values.shape[0]
+    rows = lax.broadcasted_iota(jnp.int32, values.shape, 0)
+    edge = 0 if by < 0 else width - 1
+    outside = rows == edge
+    for frame in range(1, count // width):
+        outside = outside | (rows == frame * width + edge)
+    moved = pltpu.roll(values, 1 if by < 0 else count - 1, 0)
+    return jnp.where(outside, 0.0, moved)
+
+
+def transposed_slices(values, width, share, store):
+    frames = values.shape[0] // width
+    channels = values.shape[1]
+    for frame in range(frames):
+        part = values[frame * width : (frame + 1) * width]
+        part = jnp.concatenate([part, jnp.zeros((LANES - width, channels), part.dtype)], axis=0)
+        turned = part.T.astype(jnp.bfloat16)
+        for piece in range(channels // share):
+            store(piece, frame * share, turned[piece * share : (piece + 1) * share])
+
+
+def kernel(
+    space, time, width, factor,
+    x_ref, g_ref, w_hbm, ig_ref, wg_ref,
+    w_ref, xbuf, ubuf, xts, uts, xrecv, urecv, xb,
+    w_sem, hx_send, hx_recv, hu_send, hu_recv,
+    x1_send, x1_recv, x2_send, x2_recv, u1_send, u1_recv, u2_send, u2_recv,
+):
+    z = lax.axis_index("space")
+    t = lax.axis_index("tm")
+    cells, cin = x_ref.shape
+    cout = g_ref.shape[1]
+    in_share, out_share = cin // time, cout // space
+    frames = cells // width
+    lanes = space * LANES
+    weight_copy = pltpu.make_async_copy(w_hbm, w_ref, w_sem)
+    weight_copy.start()
+
+    below, above = z > 0, z < space - 1
+    early, late = t > 0, t < time - 1
+    diagonals = (
+        (below & early, -1, -1), (below & late, -1, 1), (above & early, 1, -1), (above & late, 1, 1),
+    )
+
+    def at(dz, dt):
+        return {"space": z + dz, "tm": t + dt}
+
+    barrier = pltpu.get_barrier_semaphore()
+    for step in range(1, space):
+        pl.semaphore_signal(
+            barrier, 1, device_id={"space": lax.rem(z + step, space), "tm": t}, device_id_type=MESH
+        )
+    for step in range(1, time):
+        pl.semaphore_signal(
+            barrier, 1, device_id={"space": z, "tm": lax.rem(t + step, time)}, device_id_type=MESH
+        )
+    for there, dz, dt in diagonals:
+        @pl.when(there)
+        def _(dz=dz, dt=dt):
+            pl.semaphore_signal(barrier, 1, device_id=at(dz, dt), device_id_type=MESH)
+
+    own = x_ref[...]
+    xbuf[1, cells:] = own
+
+    def keep_x(piece, row, block):
+        xts[piece, pl.ds(row, in_share)] = block
+
+    transposed_slices(own.astype(jnp.float32), width, in_share, keep_x)
+    xrecv[z, t] = xts[t]
+    urecv[:, time * lanes :] = jnp.zeros((frames * out_share, lanes), jnp.bfloat16)
+    block = (cells, cin)
+
+    @pl.when(jnp.logical_not(early))
+    def _():
+        for row in range(3):
+            xbuf[row, :cells] = jnp.zeros(block, jnp.bfloat16)
+
+    @pl.when(jnp.logical_not(late))
+    def _():
+        for row in range(3):
+            ubuf[row, cells:] = jnp.zeros((cells, cout), jnp.bfloat16)
+
+    for missing, row in ((jnp.logical_not(below), 0), (jnp.logical_not(above), 2)):
+        @pl.when(missing)
+        def _(row=row):
+            xbuf[row] = jnp.zeros((2 * cells, cin), jnp.bfloat16)
+            ubuf[row] = jnp.zeros((2 * cells, cout), jnp.bfloat16)
+
+    beside = (z + space - 1) // space + (2 * space - 2 - z) // space
+    around = (t + time - 1) // time + (2 * time - 2 - t) // time
+    pl.semaphore_wait(barrier, space + time - 2 + beside * around)
+
+    def halo(source, buf, send, recv, slot, row, half, there, dz, dt):
+        copy = pltpu.make_async_remote_copy(
+            src_ref=source,
+            dst_ref=buf.at[row, pl.ds(half * cells, cells)],
+            send_sem=send.at[slot],
+            recv_sem=recv.at[slot],
+            device_id=at(dz, dt),
+            device_id_type=MESH,
+        )
+        return there, copy
+
+    def start(pair):
+        @pl.when(pair[0])
+        def _():
+            pair[1].start()
+
+    def received(here, copy):
+        @pl.when(here)
+        def _():
+            copy.wait_recv()
+
+    x_halo = (
+        (halo(x_ref, xbuf, hx_send, hx_recv, 0, 1, 0, late, 0, 1), early),
+        (halo(x_ref, xbuf, hx_send, hx_recv, 1, 0, 1, above, 1, 0), below),
+        (halo(x_ref, xbuf, hx_send, hx_recv, 2, 2, 1, below, -1, 0), above),
+        (halo(x_ref, xbuf, hx_send, hx_recv, 3, 0, 0, above & late, 1, 1), below & early),
+        (halo(x_ref, xbuf, hx_send, hx_recv, 4, 2, 0, below & late, -1, 1), above & early),
+    )
+    for pair, _ in x_halo:
+        start(pair)
+
+    def exchange(source, target, send, recv, slot, mine, device):
+        return pltpu.make_async_remote_copy(
+            src_ref=source, dst_ref=target, send_sem=send.at[slot], recv_sem=recv.at[slot],
+            device_id=device, device_id_type=MESH,
+        )
+
+    x1, x2, u1, u2 = [], [], [], []
+    for step in range(1, time):
+        other = lax.rem(t + step, time)
+        x1.append(exchange(xts.at[other], xrecv.at[z, t], x1_send, x1_recv, step - 1, t,
+                           {"space": z, "tm": other}))
+        window = urecv.at[:, pl.ds(pl.multiple_of(t * lanes, LANES), lanes)]
+        u2.append(exchange(window, window, u2_send, u2_recv, step - 1, t, {"space": z, "tm": other}))
+    for step in range(1, space):
+        other = lax.rem(z + step, space)
+        x2.append(exchange(xrecv.at[z], xrecv.at[z], x2_send, x2_recv, step - 1, z,
+                           {"space": other, "tm": t}))
+        window = urecv.at[:, pl.ds(pl.multiple_of(t * lanes + z * LANES, LANES), LANES)]
+        u1.append(exchange(uts.at[other], window, u1_send, u1_recv, step - 1, z,
+                           {"space": other, "tm": t}))
+    for copy in x1:
+        copy.start()
+
+    def taps(buf, row, tap_row, forward, totals):
+        for depth in range(3):
+            offset = (depth if forward else 2 - depth) * width
+            window = buf[row, offset : offset + cells]
+            for col in range(3):
+                tap = w_ref[(depth * 3 + tap_row) * 3 + col]
+                product = lax.dot_general(
+                    window, tap, (((1,), (0 if forward else 1,)), ((), ())),
+                    preferred_element_type=jnp.float32,
+                )
+                totals[col] = product if totals[col] is None else totals[col] + product
+
+    weight_copy.wait()
+    sums = [None, None, None]
+    received(x_halo[0][1], x_halo[0][0][1])
+    taps(xbuf, 1, 1, True, sums)
+    for copy in x1:
+        copy.wait_recv()
+    for copy in x2:
+        copy.start()
+    for (_, copy), here in x_halo[1:]:
+        received(here, copy)
+    taps(xbuf, 0, 0, True, sums)
+    taps(xbuf, 2, 2, True, sums)
+    outputs = shifted_rows(sums[0], -1, width) + sums[1] + shifted_rows(sums[2], 1, width)
+    logistic = jax.nn.sigmoid(outputs)
+    derivative = logistic * (1.0 + outputs * (1.0 - logistic))
+    upstream = (g_ref[...].astype(jnp.float32) * derivative).astype(jnp.bfloat16)
+    ubuf[1, :cells] = upstream
+
+    def keep_u(piece, row, block):
+        uts[piece, pl.ds(row, out_share)] = block
+
+    transposed_slices(upstream.astype(jnp.float32), width, out_share, keep_u)
+    urecv[:, pl.ds(pl.multiple_of(t * lanes + z * LANES, LANES), LANES)] = uts[z]
+    for copy in u1:
+        copy.start()
+    u_own = ubuf.at[1, pl.ds(0, cells)]
+    u_halo = (
+        (halo(u_own, ubuf, hu_send, hu_recv, 0, 1, 1, early, 0, -1), late),
+        (halo(u_own, ubuf, hu_send, hu_recv, 1, 0, 0, above, 1, 0), below),
+        (halo(u_own, ubuf, hu_send, hu_recv, 2, 2, 0, below, -1, 0), above),
+        (halo(u_own, ubuf, hu_send, hu_recv, 3, 0, 1, above & early, 1, -1), below & late),
+        (halo(u_own, ubuf, hu_send, hu_recv, 4, 2, 1, below & early, -1, -1), above & late),
+    )
+    for pair, _ in u_halo:
+        start(pair)
+
+    for copy in x2:
+        copy.wait_recv()
+    for pair_at in range(time):
+        base = pair_at * lanes
+        nothing = jnp.zeros((frames * in_share, LANES), jnp.bfloat16)
+        for col in range(3):
+            xb[col, :, base : base + LANES] = nothing
+            xb[6 + col, :, base + lanes - LANES : base + lanes] = nothing
+        for row in range(space):
+            held = xrecv[row, pair_at]
+            wide = held.astype(jnp.float32)
+            moved = (
+                pltpu.roll(wide, 1, 1).astype(jnp.bfloat16),
+                held,
+                pltpu.roll(wide, LANES - 1, 1).astype(jnp.bfloat16),
+            )
+            for tap_row in range(3):
+                place = row - tap_row + 1
+                if 0 <= place < space:
+                    for col in range(3):
+                        xb[tap_row * 3 + col, :, base + place * LANES : base + (place + 1) * LANES] = moved[col]
+
+    for copy in u1:
+        copy.wait_recv()
+    for copy in u2:
+        copy.start()
+
+    sums = [None, None, None]
+    received(u_halo[0][1], u_halo[0][0][1])
+    taps(ubuf, 1, 1, False, sums)
+    for (_, copy), here in u_halo[1:]:
+        received(here, copy)
+    taps(ubuf, 0, 2, False, sums)
+    taps(ubuf, 2, 0, False, sums)
+    total = shifted_rows(sums[0], 1, width) + sums[1] + shifted_rows(sums[2], -1, width)
+    ig_ref[...] = total.astype(jnp.bfloat16)
+
+    for copy in u2:
+        copy.wait_recv()
+    both = jnp.concatenate([urecv[:, : time * lanes], urecv[:, lanes:]], axis=0)
+    for tap_row in range(3):
+        left = xb[tap_row * 3 : tap_row * 3 + 3].reshape(3 * frames * in_share, time * lanes)
+        grads = lax.dot_general(
+            left, both, (((1,), (1,)), ((), ())), preferred_element_type=jnp.float32
+        ) * factor
+        grads = grads.reshape(3, frames, in_share, 2 * frames * out_share)
+        for col in range(3):
+            joined = grads[col, 0, :, : 3 * out_share] + grads[col, 1, :, out_share:]
+            for depth in range(3):
+                lag = 2 - depth
+                wg_ref[(depth * 3 + tap_row) * 3 + col] = joined[:, lag * out_share : (lag + 1) * out_share]
+
+    for copy in x1 + x2 + u1 + u2:
+        copy.wait_send()
+    for pair, _ in x_halo + u_halo:
+        @pl.when(pair[0])
+        def _(copy=pair[1]):
+            copy.wait_send()
+
+
+def gathered(space, time, inputs, cotangent, weight):
+    frames, _, width, cin = inputs.shape
+    cout = cotangent.shape[3]
+    cells = frames * width
+    in_share, out_share = cin // time, cout // space
+    lanes = space * LANES
+    factor = 1.0 / math.sqrt(cells * space * time)
+    vmem = pl.BlockSpec(memory_space=pltpu.VMEM)
+    dma = pltpu.SemaphoreType.DMA
+    bf16 = jnp.bfloat16
+    input_grad, weight_grad = pl.pallas_call(
+        functools.partial(kernel, space, time, width, factor),
+        out_shape=(
+            jax.ShapeDtypeStruct((cells, cin), bf16),
+            jax.ShapeDtypeStruct((27, in_share, out_share), jnp.float32),
+        ),
+        in_specs=[vmem, vmem, pl.BlockSpec(memory_space=pl.ANY)],
+        out_specs=(vmem, vmem),
+        scratch_shapes=[
+            pltpu.VMEM((27, cin, cout), bf16),
+            pltpu.VMEM((3, 2 * cells, cin), bf16),
+            pltpu.VMEM((3, 2 * cells, cout), bf16),
+            pltpu.VMEM((time, frames * in_share, LANES), bf16),
+            pltpu.VMEM((space, frames * out_share, LANES), bf16),
+            pltpu.VMEM((space, time, frames * in_share, LANES), bf16),
+            pltpu.VMEM((frames * out_share, (time + 1) * lanes), bf16),
+            pltpu.VMEM((9, frames * in_share, time * lanes), bf16),
+            dma,
+            dma((5,)), dma((5,)), dma((5,)), dma((5,)),
+            dma((time - 1,)), dma((time - 1,)), dma((space - 1,)), dma((space - 1,)),
+            dma((space - 1,)), dma((space - 1,)), dma((time - 1,)), dma((time - 1,)),
+        ],
+        compiler_params=pltpu.CompilerParams(
+            collective_id=0, has_side_effects=True, vmem_limit_bytes=62 * 1024 * 1024
+        ),
+    )(inputs.reshape(cells, cin), cotangent.reshape(cells, cout), weight.reshape(27, cin, cout))
+    return (
+        input_grad.reshape(inputs.shape),
+        weight_grad.reshape(3, 3, 3, in_share, out_share),
+    )
+
+
+def local(space, time, inputs, cotangent, weight):
+    frames, rows, width, cin = inputs.shape
+    cout = cotangent.shape[3]
+    slices = 2 * frames * rows * width * space * time * (cin // time + cout // space)
+    partials = 4 * 27 * cin * cout
+    fits = (
+        frames == 2
+        and rows == 1
+        and width < LANES
+        and width % 16 == 0
+        and space > 1
+        and time > 1
+        and (cin // time) % 16 == 0
+        and (cout // space) % 16 == 0
+    )
+    if fits and slices < partials:
+        return gathered(space, time, inputs, cotangent, weight)
+    return reduced(inputs, cotangent, weight)
+
+
 def solution(mesh):
     placed = (P(("rep", "tm"), "space", None, None), P(("rep", "tm"), "space", None, None), P())
     return jax.shard_map(
-        local,
+        functools.partial(local, mesh.shape["space"], mesh.shape["tm"]),
         mesh=mesh,
         in_specs=placed,
         out_specs=(

time: 197 us -> 35.7 us (0.18)
  waiting for transfers between devices: 119 us -> 0 us
  Pallas kernels: 0 us -> 31.3 us
  matrix products: 30.4 us -> 0 us
  starting transfers between devices: 15.6 us -> 0 us
  between operations: 15 us -> 0.64 us
  local copies, waits for them, and re-layouts: 13.5 us -> 3.51 us
    reduce_scatter x2 -> x0, waiting for transfers between devices: 90.1 us -> none  [the longest x1 66.3 us: local(): lax.psum_scatter(blocks, 'space', scatter_dimension=0, tiled=True)]
    pallas_call x0 -> x1, Pallas kernels: none -> 31.3 us  [gathered(): pl.pallas_call(functools.partial(kernel, space, time, width, factor), out...]
    dot_general x81 -> x0, matrix products: 30.4 us -> none  [the longest x27 14.2 us: local(): lax.dot_general(returned, weight[depth_tap, row_tap, col_tap], (((1,), (1...]
    ppermute x6 -> x0, waiting for transfers between devices: 29.2 us -> none  [the longest x2 14.1 us: extended_2(): lax.ppermute(head, axis, [((i + 1) % count, i) for i in range(ends)])]
    ppermute x6 -> x0, starting transfers between devices: 15.5 us -> none  [the longest x2 6.55 us: passed_along(): return lax.ppermute(array, axis, pairs)]
    transpose x2 -> x0, local copies, waits for them, and re-layouts: 5.3 us -> none  [the longest x1 2.71 us: local(): blocks.transpose(2, 0, 1, 3)]
    reshape x1 -> x0, local copies, waits for them, and re-layouts: 2.59 us -> none  [local(): blocks = spatial_sum.reshape(27, time_size, in_share, out_share)]
    slice x7 -> x0, local copies, waits for them, and re-layouts: 2.58 us -> none  [the longest x3 2.29 us: local(): following[2 - depth_tap:2 - depth_tap + frame_count, 2 - row_tap:2 - row_...]
  transfers between devices with their start and end apart: 8 -> 0, of which waited for: 8 -> 0; matrix products, arithmetic and copies ran while one was open for 9% -> 0% of each run, Pallas kernels for 0% -> 0%
where the time goes in v1:
time: 35.7 us; the launch traced here: 35.4 us
  Pallas kernels  31.3 us (88%)
  local copies, waits for them, and re-layouts  3.51 us (10%)
  between operations  0.64 us (2%)
    pallas_call x1, Pallas kernels, gathered(): pl.pallas_call(functools.partial(kernel, space, time, width, factor), out...  31.3 us
    unnamed x2, local copies, waits for them, and re-layouts  3.51 us

profile of v1, /device:TPU:1, one launch (start us, length us, event | category | flops | bytes accessed | tf_op | source)
XLA Modules:
  0.0 35.4 jit_solution(1887771260990839326)
XLA Ops:
  0.6 31.3 %shard_map.50 = (bf16[192,192]{1,0:T(8,128)(2,1)}, f32[27,48,48]{2,1,0:T(8,128)}) custom-call(bf16[192,192]{1,0:T(8,128)(2,1)} %bitcast.9, bf16[192,192]{1,0:T(8,128)(2,1)} %bitcast.10, bf16[27,192,192]{2,1,0:T(8,128)(2,1)} %bitcast.7), custom_call_target="tpu_custom_call" | custom-call | tf_op jit(solution)/shard_map/pallas_call | solution.py:380
  31.9 1.5 %copy.8 = bf16[2,1,96,192]{3,2,1,0:T(8,128)(2,1)} copy(bf16[2,1,96,192]{3,2,1,0:T(8,128)(2,1)} %bitcast.11) | data formatting | bytes 147456
  33.5 2.0 %copy.9 = f32[3,3,3,48,48]{4,3,2,1,0:T(8,128)} copy(f32[3,3,3,48,48]{4,3,2,1,0:T(8,128)} %bitcast.8) | data formatting | bytes 497664

commit v2 on v1

--- a/solution.py
+++ b/solution.py
@@ -137,9 +137,9 @@
 def kernel(
     space, time, width, factor,
     x_ref, g_ref, w_hbm, ig_ref, wg_ref,
-    w_ref, xbuf, ubuf, xts, uts, xrecv, urecv, xb,
+    w_ref, xbuf, ubuf, xpack, upack, xheld, uheld, xts, uts, xrecv, urecv, xb,
     w_sem, hx_send, hx_recv, hu_send, hu_recv,
-    x1_send, x1_recv, x2_send, x2_recv, u1_send, u1_recv, u2_send, u2_recv,
+    x1_send, x1_recv, up_send, up_recv, down_send, down_recv, u1_send, u1_recv, u2_send, u2_recv,
 ):
     z = lax.axis_index("space")
     t = lax.axis_index("tm")
@@ -153,9 +153,7 @@
 
     below, above = z > 0, z < space - 1
     early, late = t > 0, t < time - 1
-    diagonals = (
-        (below & early, -1, -1), (below & late, -1, 1), (above & early, 1, -1), (above & late, 1, 1),
-    )
+    partner = t + 1 - 2 * lax.rem(t, 2)
 
     def at(dz, dt):
         return {"space": z + dz, "tm": t + dt}
@@ -169,12 +167,18 @@
         pl.semaphore_signal(
             barrier, 1, device_id={"space": z, "tm": lax.rem(t + step, time)}, device_id_type=MESH
         )
-    for there, dz, dt in diagonals:
+    for there, dz, dt in (
+        (below & early, -1, -1), (below & late, -1, 1), (above & early, 1, -1), (above & late, 1, 1),
+    ):
         @pl.when(there)
         def _(dz=dz, dt=dt):
             pl.semaphore_signal(barrier, 1, device_id=at(dz, dt), device_id_type=MESH)
 
+    def side_by_side(values):
+        return jnp.concatenate([values[n * width : (n + 1) * width] for n in range(frames)], axis=1)
+
     own = x_ref[...]
+    xpack[...] = side_by_side(own)
     xbuf[1, cells:] = own
 
     def keep_x(piece, row, block):
@@ -183,12 +187,16 @@
     transposed_slices(own.astype(jnp.float32), width, in_share, keep_x)
     xrecv[z, t] = xts[t]
     urecv[:, time * lanes :] = jnp.zeros((frames * out_share, lanes), jnp.bfloat16)
-    block = (cells, cin)
+    nothing = jnp.zeros((frames * in_share, LANES), jnp.bfloat16)
+    for pair_at in range(time):
+        for col in range(3):
+            xb[col, :, pair_at * lanes : pair_at * lanes + LANES] = nothing
+            xb[6 + col, :, (pair_at + 1) * lanes - LANES : (pair_at + 1) * lanes] = nothing
 
     @pl.when(jnp.logical_not(early))
     def _():
         for row in range(3):
-            xbuf[row, :cells] = jnp.zeros(block, jnp.bfloat16)
+            xbuf[row, :cells] = jnp.zeros((cells, cin), jnp.bfloat16)
 
     @pl.when(jnp.logical_not(late))
     def _():
@@ -205,62 +213,84 @@
     around = (t + time - 1) // time + (2 * time - 2 - t) // time
     pl.semaphore_wait(barrier, space + time - 2 + beside * around)
 
-    def halo(source, buf, send, recv, slot, row, half, there, dz, dt):
-        copy = pltpu.make_async_remote_copy(
-            src_ref=source,
-            dst_ref=buf.at[row, pl.ds(half * cells, cells)],
-            send_sem=send.at[slot],
-            recv_sem=recv.at[slot],
-            device_id=at(dz, dt),
-            device_id_type=MESH,
-        )
-        return there, copy
-
-    def start(pair):
-        @pl.when(pair[0])
-        def _():
-            pair[1].start()
-
-    def received(here, copy):
-        @pl.when(here)
-        def _():
-            copy.wait_recv()
-
-    x_halo = (
-        (halo(x_ref, xbuf, hx_send, hx_recv, 0, 1, 0, late, 0, 1), early),
-        (halo(x_ref, xbuf, hx_send, hx_recv, 1, 0, 1, above, 1, 0), below),
-        (halo(x_ref, xbuf, hx_send, hx_recv, 2, 2, 1, below, -1, 0), above),
-        (halo(x_ref, xbuf, hx_send, hx_recv, 3, 0, 0, above & late, 1, 1), below & early),
-        (halo(x_ref, xbuf, hx_send, hx_recv, 4, 2, 0, below & late, -1, 1), above & early),
-    )
-    for pair, _ in x_halo:
-        start(pair)
-
-    def exchange(source, target, send, recv, slot, mine, device):
+    def remote(source, target, send, recv, slot, device):
         return pltpu.make_async_remote_copy(
             src_ref=source, dst_ref=target, send_sem=send.at[slot], recv_sem=recv.at[slot],
             device_id=device, device_id_type=MESH,
         )
 
-    x1, x2, u1, u2 = [], [], [], []
+    def halos(pack, held, send, recv, ahead, there, here):
+        cases = (
+            (0, ahead, there, here),
+            (1, 0, above, below),
+            (-1, 0, below, above),
+            (1, ahead, above & there, below & here),
+            (-1, ahead, below & there, above & here),
+        )
+        return [
+            (sent, got, 1 - dz, dt != 0,
+             remote(pack, held.at[slot], send, recv, slot, at(dz, dt)))
+            for slot, (dz, dt, sent, got) in enumerate(cases)
+        ]
+
+    def start_if(there, copy):
+        @pl.when(there)
+        def _():
+            copy.start()
+
+    def unpacked(halo, held, slot, buf, own_half):
+        _, got, row, other_time, copy = halo
+        half = 1 - own_half if other_time else own_half
+        channels = buf.shape[2]
+
+        @pl.when(got)
+        def _():
+            copy.wait_recv()
+            for n in range(frames):
+                place = half * cells + n * width
+                buf[row, place : place + width] = held[slot, :, n * channels : (n + 1) * channels]
+
+    x_halo = halos(xpack, xheld, hx_send, hx_recv, 1, late, early)
+    for sent, _, _, _, copy in x_halo:
+        start_if(sent, copy)
+
+    x1, u1 = [], []
     for step in range(1, time):
         other = lax.rem(t + step, time)
-        x1.append(exchange(xts.at[other], xrecv.at[z, t], x1_send, x1_recv, step - 1, t,
-                           {"space": z, "tm": other}))
-        window = urecv.at[:, pl.ds(pl.multiple_of(t * lanes, LANES), lanes)]
-        u2.append(exchange(window, window, u2_send, u2_recv, step - 1, t, {"space": z, "tm": other}))
+        x1.append(remote(xts.at[other], xrecv.at[z, t], x1_send, x1_recv, step - 1,
+                         {"space": z, "tm": other}))
     for step in range(1, space):
         other = lax.rem(z + step, space)
-        x2.append(exchange(xrecv.at[z], xrecv.at[z], x2_send, x2_recv, step - 1, z,
-                           {"space": other, "tm": t}))
         window = urecv.at[:, pl.ds(pl.multiple_of(t * lanes + z * LANES, LANES), LANES)]
-        u1.append(exchange(uts.at[other], window, u1_send, u1_recv, step - 1, z,
-                           {"space": other, "tm": t}))
+        u1.append(remote(uts.at[other], window, u1_send, u1_recv, step - 1,
+                         {"space": other, "tm": t}))
     for copy in x1:
         copy.start()
 
-    def taps(buf, row, tap_row, forward, totals):
-        for depth in range(3):
+    hops = []
+    for step in range(space - 1):
+        up, down = xrecv.at[z - step], xrecv.at[z + step]
+        hops.append((
+            (above & (z >= step), below & (z > step), z - 1 - step,
+             remote(up, up, up_send, up_recv, step, at(1, 0))),
+            (below & (z + step < space), above & (z + step + 1 < space), z + 1 + step,
+             remote(down, down, down_send, down_recv, step, at(-1, 0))),
+        ))
+
+    def gather(source_time, slot, device_time):
+        window = urecv.at[:, pl.ds(pl.multiple_of(source_time * lanes, LANES), lanes)]
+        return remote(window, window, u2_send, u2_recv, slot, {"space": z, "tm": device_time})
+
+    couples = time // 2
+    first, second = [gather(t, 0, partner)], []
+    for step in range(1, couples):
+        first.append(gather(t, step, lax.rem(t + 2 * step, time)))
+        came_from = lax.rem(t + time - 2 * step, time)
+        second.append(gather(came_from, couples + step - 1, partner))
+
+    def taps(buf, row, depths, forward, totals):
+        tap_row = row if forward else 2 - row
+        for depth in depths:
             offset = (depth if forward else 2 - depth) * width
             window = buf[row, offset : offset + cells]
             for col in range(3):
@@ -271,51 +301,8 @@
                 )
                 totals[col] = product if totals[col] is None else totals[col] + product
 
-    weight_copy.wait()
-    sums = [None, None, None]
-    received(x_halo[0][1], x_halo[0][0][1])
-    taps(xbuf, 1, 1, True, sums)
-    for copy in x1:
-        copy.wait_recv()
-    for copy in x2:
-        copy.start()
-    for (_, copy), here in x_halo[1:]:
-        received(here, copy)
-    taps(xbuf, 0, 0, True, sums)
-    taps(xbuf, 2, 2, True, sums)
-    outputs = shifted_rows(sums[0], -1, width) + sums[1] + shifted_rows(sums[2], 1, width)
-    logistic = jax.nn.sigmoid(outputs)
-    derivative = logistic * (1.0 + outputs * (1.0 - logistic))
-    upstream = (g_ref[...].astype(jnp.float32) * derivative).astype(jnp.bfloat16)
-    ubuf[1, :cells] = upstream
-
-    def keep_u(piece, row, block):
-        uts[piece, pl.ds(row, out_share)] = block
-
-    transposed_slices(upstream.astype(jnp.float32), width, out_share, keep_u)
-    urecv[:, pl.ds(pl.multiple_of(t * lanes + z * LANES, LANES), LANES)] = uts[z]
-    for copy in u1:
-        copy.start()
-    u_own = ubuf.at[1, pl.ds(0, cells)]
-    u_halo = (
-        (halo(u_own, ubuf, hu_send, hu_recv, 0, 1, 1, early, 0, -1), late),
-        (halo(u_own, ubuf, hu_send, hu_recv, 1, 0, 0, above, 1, 0), below),
-        (halo(u_own, ubuf, hu_send, hu_recv, 2, 2, 0, below, -1, 0), above),
-        (halo(u_own, ubuf, hu_send, hu_recv, 3, 0, 1, above & early, 1, -1), below & late),
-        (halo(u_own, ubuf, hu_send, hu_recv, 4, 2, 1, below & early, -1, -1), above & late),
-    )
-    for pair, _ in u_halo:
-        start(pair)
-
-    for copy in x2:
-        copy.wait_recv()
-    for pair_at in range(time):
-        base = pair_at * lanes
-        nothing = jnp.zeros((frames * in_share, LANES), jnp.bfloat16)
-        for col in range(3):
-            xb[col, :, base : base + LANES] = nothing
-            xb[6 + col, :, base + lanes - LANES : base + lanes] = nothing
-        for row in range(space):
+    def placed(row):
+        for pair_at in range(time):
             held = xrecv[row, pair_at]
             wide = held.astype(jnp.float32)
             moved = (
@@ -325,26 +312,102 @@
             )
             for tap_row in range(3):
                 place = row - tap_row + 1
-                if 0 <= place < space:
+
+                @pl.when((place >= 0) & (place < space))
+                def _(tap_row=tap_row, place=place):
+                    start = pl.multiple_of(pair_at * lanes + place * LANES, LANES)
                     for col in range(3):
-                        xb[tap_row * 3 + col, :, base + place * LANES : base + (place + 1) * LANES] = moved[col]
+                        xb[tap_row * 3 + col, :, pl.ds(start, LANES)] = moved[col]
+
+    def hop_received(step):
+        for _, got, _, copy in hops[step]:
+            @pl.when(got)
+            def _(copy=copy):
+                copy.wait_recv()
+
+    def hop_placed(step):
+        for _, got, row, _ in hops[step]:
+            @pl.when(got)
+            def _(row=row):
+                placed(row)
+
+    weight_copy.wait()
+    sums = [None, None, None]
+    taps(xbuf, 1, (2,), True, sums)
+    unpacked(x_halo[0], xheld, 0, xbuf, 1)
+    taps(xbuf, 1, (0, 1), True, sums)
+    unpacked(x_halo[1], xheld, 1, xbuf, 1)
+    taps(xbuf, 0, (2,), True, sums)
+    unpacked(x_halo[2], xheld, 2, xbuf, 1)
+    taps(xbuf, 2, (2,), True, sums)
+    unpacked(x_halo[3], xheld, 3, xbuf, 1)
+    taps(xbuf, 0, (0, 1), True, sums)
+    unpacked(x_halo[4], xheld, 4, xbuf, 1)
+    for copy in x1:
+        copy.wait_recv()
+    for sent, _, _, copy in hops[0]:
+        start_if(sent, copy)
+    taps(xbuf, 2, (0, 1), True, sums)
+    outputs = shifted_rows(sums[0], -1, width) + sums[1] + shifted_rows(sums[2], 1, width)
+    logistic = jax.nn.sigmoid(outputs)
+    derivative = logistic * (1.0 + outputs * (1.0 - logistic))
+    upstream = (g_ref[...].astype(jnp.float32) * derivative).astype(jnp.bfloat16)
+
+    def keep_u(piece, row, block):
+        uts[piece, pl.ds(row, out_share)] = block
+
+    transposed_slices(upstream.astype(jnp.float32), width, out_share, keep_u)
+    upack[...] = side_by_side(upstream)
+    for copy in u1:
+        copy.start()
+    u_halo = halos(upack, uheld, hu_send, hu_recv, -1, early, late)
+    for sent, _, _, _, copy in u_halo:
+        start_if(sent, copy)
+    ubuf[1, :cells] = upstream
+    urecv[:, pl.ds(pl.multiple_of(t * lanes + z * LANES, LANES), LANES)] = uts[z]
+    hop_received(0)
+    if space > 2:
+        for sent, _, _, copy in hops[1]:
+            start_if(sent, copy)
+    placed(z)
+    hop_placed(0)
 
     for copy in u1:
         copy.wait_recv()
-    for copy in u2:
+    for copy in first:
         copy.start()
 
+    for step in range(1, space - 1):
+        hop_received(step)
+        if step + 1 < space - 1:
+            for sent, _, _, copy in hops[step + 1]:
+                start_if(sent, copy)
+        if step + 1 < space - 1:
+            hop_placed(step)
+
     sums = [None, None, None]
-    received(u_halo[0][1], u_halo[0][0][1])
-    taps(ubuf, 1, 1, False, sums)
-    for (_, copy), here in u_halo[1:]:
-        received(here, copy)
-    taps(ubuf, 0, 2, False, sums)
-    taps(ubuf, 2, 0, False, sums)
+    taps(ubuf, 1, (2,), False, sums)
+    unpacked(u_halo[0], uheld, 0, ubuf, 0)
+    taps(ubuf, 1, (0, 1), False, sums)
+    unpacked(u_halo[1], uheld, 1, ubuf, 0)
+    taps(ubuf, 0, (2,), False, sums)
+    unpacked(u_halo[2], uheld, 2, ubuf, 0)
+    taps(ubuf, 2, (2,), False, sums)
+    for copy in first[1:]:
+        copy.wait_recv()
+    for copy in second:
+        copy.start()
+    unpacked(u_halo[3], uheld, 3, ubuf, 0)
+    taps(ubuf, 0, (0, 1), False, sums)
+    unpacked(u_halo[4], uheld, 4, ubuf, 0)
+    taps(ubuf, 2, (0, 1), False, sums)
     total = shifted_rows(sums[0], 1, width) + sums[1] + shifted_rows(sums[2], -1, width)
     ig_ref[...] = total.astype(jnp.bfloat16)
-
-    for copy in u2:
+    if space > 2:
+        hop_placed(space - 2)
+
+    first[0].wait_recv()
+    for copy in second:
         copy.wait_recv()
     both = jnp.concatenate([urecv[:, : time * lanes], urecv[:, lanes:]], axis=0)
     for tap_row in range(3):
@@ -359,12 +422,28 @@
                 lag = 2 - depth
                 wg_ref[(depth * 3 + tap_row) * 3 + col] = joined[:, lag * out_share : (lag + 1) * out_share]
 
-    for copy in x1 + x2 + u1 + u2:
+    for copy in x1 + u1 + first + second:
         copy.wait_send()
-    for pair, _ in x_halo + u_halo:
-        @pl.when(pair[0])
-        def _(copy=pair[1]):
+    for sent, _, _, _, copy in x_halo + u_halo:
+        @pl.when(sent)
+        def _(copy=copy):
             copy.wait_send()
+    for pair in hops:
+        for sent, _, _, copy in pair:
+            @pl.when(sent)
+            def _(copy=copy):
+                copy.wait_send()
+
+
+def written(ig_ref, wg_ref, ig_out, wg_out, sems):
+    copies = [
+        pltpu.make_async_copy(wg_ref, wg_out, sems.at[0]),
+        pltpu.make_async_copy(ig_ref, ig_out, sems.at[1]),
+    ]
+    for copy in copies:
+        copy.start()
+    for copy in copies:
+        copy.wait()
 
 
 def gathered(space, time, inputs, cotangent, weight):
@@ -389,6 +468,10 @@
             pltpu.VMEM((27, cin, cout), bf16),
             pltpu.VMEM((3, 2 * cells, cin), bf16),
             pltpu.VMEM((3, 2 * cells, cout), bf16),
+            pltpu.VMEM((width, frames * cin), bf16),
+            pltpu.VMEM((width, frames * cout), bf16),
+            pltpu.VMEM((5, width, frames * cin), bf16),
+            pltpu.VMEM((5, width, frames * cout), bf16),
             pltpu.VMEM((time, frames * in_share, LANES), bf16),
             pltpu.VMEM((space, frames * out_share, LANES), bf16),
             pltpu.VMEM((space, time, frames * in_share, LANES), bf16),
@@ -396,13 +479,25 @@
             pltpu.VMEM((9, frames * in_share, time * lanes), bf16),
             dma,
             dma((5,)), dma((5,)), dma((5,)), dma((5,)),
-            dma((time - 1,)), dma((time - 1,)), dma((space - 1,)), dma((space - 1,)),
+            dma((time - 1,)), dma((time - 1,)),
+            dma((space - 1,)), dma((space - 1,)), dma((space - 1,)), dma((space - 1,)),
             dma((space - 1,)), dma((space - 1,)), dma((time - 1,)), dma((time - 1,)),
         ],
         compiler_params=pltpu.CompilerParams(
             collective_id=0, has_side_effects=True, vmem_limit_bytes=62 * 1024 * 1024
         ),
     )(inputs.reshape(cells, cin), cotangent.reshape(cells, cout), weight.reshape(27, cin, cout))
+    anywhere = pl.BlockSpec(memory_space=pl.ANY)
+    input_grad, weight_grad = pl.pallas_call(
+        written,
+        out_shape=(
+            jax.ShapeDtypeStruct(input_grad.shape, bf16),
+            jax.ShapeDtypeStruct(weight_grad.shape, jnp.float32),
+        ),
+        in_specs=[vmem, vmem],
+        out_specs=(anywhere, anywhere),
+        scratch_shapes=[dma((2,))],
+    )(input_grad, weight_grad)
     return (
         input_grad.reshape(inputs.shape),
         weight_grad.reshape(3, 3, 3, in_share, out_share),
@@ -420,7 +515,7 @@
         and width < LANES
         and width % 16 == 0
         and space > 1
-        and time > 1
+        and time % 2 == 0
         and (cin // time) % 16 == 0
         and (cout // space) % 16 == 0
     )

time: 35.7 us -> 33.9 us (0.950)
  local copies, waits for them, and re-layouts: 3.51 us -> 0 us
  Pallas kernels: 31.3 us -> 32.7 us
    unnamed x2 -> x0, local copies, waits for them, and re-layouts: 3.51 us -> none
    pallas_call x0 -> x1, Pallas kernels: none -> 2.02 us  [gathered(): pl.pallas_call(written, out_shape=(jax.ShapeDtypeStruct(input_grad.shape,...]
    pallas_call x1, Pallas kernels: 31.3 us -> 30.7 us  [gathered(): pl.pallas_call(functools.partial(kernel, space, time, width, factor), out...]
where the time goes in v2:
time: 33.9 us; the launch traced here: 33.3 us
  Pallas kernels  32.7 us (96%)
  between operations  0.64 us (2%)
    pallas_call x1, Pallas kernels, gathered(): pl.pallas_call(functools.partial(kernel, space, time, width, factor), out...  30.7 us
    pallas_call x1, Pallas kernels, gathered(): pl.pallas_call(written, out_shape=(jax.ShapeDtypeStruct(input_grad.shape,...  2.02 us

profile of v2, /device:TPU:1, one launch (start us, length us, event | category | flops | bytes accessed | tf_op | source)
XLA Modules:
  0.0 33.3 jit_solution(9195116742141870493)
XLA Ops:
  0.6 30.7 %shard_map.50 = (bf16[192,192]{1,0:T(8,128)(2,1)}, f32[27,48,48]{2,1,0:T(8,128)}) custom-call(bf16[192,192]{1,0:T(8,128)(2,1)} %bitcast.8, bf16[192,192]{1,0:T(8,128)(2,1)} %bitcast.9, bf16[27,192,192]{2,1,0:T(8,128)(2,1)} %bitcast.7), custom_call_target="tpu_custom_call" | custom-call | tf_op jit(solution)/shard_map/pallas_call | solution.py:459
  31.3 2.0 %shard_map.51 = (bf16[192,192]{1,0:T(8,128)(2,1)}, f32[27,48,48]{2,1,0:T(8,128)}) custom-call(bf16[192,192]{1,0:T(8,128)(2,1)} %get-tuple-element.6.ig_ref, f32[27,48,48]{2,1,0:T(8,128)} %get-tuple-element.7.wg_ref), custom_call_target="tpu_custom_call" | custom-call | tf_op jit(solution)/shard_map/pallas_call | solution.py:491

commit v3 on v2

--- a/solution.py
+++ b/solution.py
@@ -136,9 +136,9 @@
 
 def kernel(
     space, time, width, factor,
-    x_ref, g_ref, w_hbm, ig_ref, wg_ref,
-    w_ref, xbuf, ubuf, xpack, upack, xheld, uheld, xts, uts, xrecv, urecv, xb,
-    w_sem, hx_send, hx_recv, hu_send, hu_recv,
+    x_hbm, g_hbm, w_hbm, ig_ref, wg_ref,
+    x_ref, g_ref, w_ref, xbuf, ubuf, xpack, upack, xheld, uheld, xts, uts, xrecv, urecv, xb,
+    load_sem, hx_send, hx_recv, hu_send, hu_recv,
     x1_send, x1_recv, up_send, up_recv, down_send, down_recv, u1_send, u1_recv, u2_send, u2_recv,
 ):
     z = lax.axis_index("space")
@@ -148,8 +148,11 @@
     in_share, out_share = cin // time, cout // space
     frames = cells // width
     lanes = space * LANES
-    weight_copy = pltpu.make_async_copy(w_hbm, w_ref, w_sem)
-    weight_copy.start()
+    input_copy = pltpu.make_async_copy(x_hbm, x_ref, load_sem.at[0])
+    weight_copy = pltpu.make_async_copy(w_hbm, w_ref, load_sem.at[1])
+    cotangent_copy = pltpu.make_async_copy(g_hbm, g_ref, load_sem.at[2])
+    for copy in (input_copy, weight_copy, cotangent_copy):
+        copy.start()
 
     below, above = z > 0, z < space - 1
     early, late = t > 0, t < time - 1
@@ -177,6 +180,7 @@
     def side_by_side(values):
         return jnp.concatenate([values[n * width : (n + 1) * width] for n in range(frames)], axis=1)
 
+    input_copy.wait()
     own = x_ref[...]
     xpack[...] = side_by_side(own)
     xbuf[1, cells:] = own
@@ -277,16 +281,28 @@
              remote(down, down, down_send, down_recv, step, at(-1, 0))),
         ))
 
-    def gather(source_time, slot, device_time):
-        window = urecv.at[:, pl.ds(pl.multiple_of(source_time * lanes, LANES), lanes)]
-        return remote(window, window, u2_send, u2_recv, slot, {"space": z, "tm": device_time})
-
     couples = time // 2
-    first, second = [gather(t, 0, partner)], []
-    for step in range(1, couples):
-        first.append(gather(t, step, lax.rem(t + 2 * step, time)))
-        came_from = lax.rem(t + time - 2 * step, time)
-        second.append(gather(came_from, couples + step - 1, partner))
+
+    def gather(piece, source_time, slot, device_time):
+        row = lax.rem(z + space - piece, space)
+        start = pl.multiple_of(source_time * lanes + row * LANES, LANES)
+        window = urecv.at[:, pl.ds(start, LANES)]
+        return remote(window, window, u2_send, u2_recv, piece * (time - 1) + slot,
+                      {"space": z, "tm": device_time})
+
+    first, second = [], []
+    for piece in range(space):
+        first.append([gather(piece, t, 0, partner)])
+        second.append([])
+        for step in range(1, couples):
+            came_from = lax.rem(t + time - 2 * step, time)
+            first[piece].append(gather(piece, t, step, lax.rem(t + 2 * step, time)))
+            second[piece].append(gather(piece, came_from, couples + step - 1, partner))
+
+    def handed_on(piece):
+        for held, copy in zip(first[piece][1:], second[piece]):
+            held.wait_recv()
+            copy.start()
 
     def taps(buf, row, depths, forward, totals):
         tap_row = row if forward else 2 - row
@@ -351,6 +367,7 @@
     outputs = shifted_rows(sums[0], -1, width) + sums[1] + shifted_rows(sums[2], 1, width)
     logistic = jax.nn.sigmoid(outputs)
     derivative = logistic * (1.0 + outputs * (1.0 - logistic))
+    cotangent_copy.wait()
     upstream = (g_ref[...].astype(jnp.float32) * derivative).astype(jnp.bfloat16)
 
     def keep_u(piece, row, block):
@@ -359,56 +376,55 @@
     transposed_slices(upstream.astype(jnp.float32), width, out_share, keep_u)
     upack[...] = side_by_side(upstream)
     for copy in u1:
+        copy.start()
+    urecv[:, pl.ds(pl.multiple_of(t * lanes + z * LANES, LANES), LANES)] = uts[z]
+    for copy in first[0]:
         copy.start()
     u_halo = halos(upack, uheld, hu_send, hu_recv, -1, early, late)
     for sent, _, _, _, copy in u_halo:
         start_if(sent, copy)
     ubuf[1, :cells] = upstream
-    urecv[:, pl.ds(pl.multiple_of(t * lanes + z * LANES, LANES), LANES)] = uts[z]
     hop_received(0)
     if space > 2:
         for sent, _, _, copy in hops[1]:
             start_if(sent, copy)
     placed(z)
+    sums = [None, None, None]
+    taps(ubuf, 1, (2,), False, sums)
+
+    for step in range(1, space):
+        u1[step - 1].wait_recv()
+        for copy in first[step]:
+            copy.start()
     hop_placed(0)
-
-    for copy in u1:
-        copy.wait_recv()
-    for copy in first:
-        copy.start()
-
     for step in range(1, space - 1):
         hop_received(step)
         if step + 1 < space - 1:
             for sent, _, _, copy in hops[step + 1]:
                 start_if(sent, copy)
-        if step + 1 < space - 1:
-            hop_placed(step)
-
-    sums = [None, None, None]
-    taps(ubuf, 1, (2,), False, sums)
+    handed_on(0)
     unpacked(u_halo[0], uheld, 0, ubuf, 0)
     taps(ubuf, 1, (0, 1), False, sums)
+    for piece in range(1, space - 1):
+        handed_on(piece)
     unpacked(u_halo[1], uheld, 1, ubuf, 0)
     taps(ubuf, 0, (2,), False, sums)
+    handed_on(space - 1)
     unpacked(u_halo[2], uheld, 2, ubuf, 0)
     taps(ubuf, 2, (2,), False, sums)
-    for copy in first[1:]:
-        copy.wait_recv()
-    for copy in second:
-        copy.start()
     unpacked(u_halo[3], uheld, 3, ubuf, 0)
     taps(ubuf, 0, (0, 1), False, sums)
     unpacked(u_halo[4], uheld, 4, ubuf, 0)
     taps(ubuf, 2, (0, 1), False, sums)
     total = shifted_rows(sums[0], 1, width) + sums[1] + shifted_rows(sums[2], -1, width)
     ig_ref[...] = total.astype(jnp.bfloat16)
-    if space > 2:
-        hop_placed(space - 2)
-
-    first[0].wait_recv()
-    for copy in second:
-        copy.wait_recv()
+    for step in range(1, space - 1):
+        hop_placed(step)
+
+    for piece in range(space):
+        first[piece][0].wait_recv()
+        for copy in second[piece]:
+            copy.wait_recv()
     both = jnp.concatenate([urecv[:, : time * lanes], urecv[:, lanes:]], axis=0)
     for tap_row in range(3):
         left = xb[tap_row * 3 : tap_row * 3 + 3].reshape(3 * frames * in_share, time * lanes)
@@ -422,7 +438,7 @@
                 lag = 2 - depth
                 wg_ref[(depth * 3 + tap_row) * 3 + col] = joined[:, lag * out_share : (lag + 1) * out_share]
 
-    for copy in x1 + u1 + first + second:
+    for copy in x1 + u1 + sum(first, []) + sum(second, []):
         copy.wait_send()
     for sent, _, _, _, copy in x_halo + u_halo:
         @pl.when(sent)
@@ -454,6 +470,7 @@
     lanes = space * LANES
     factor = 1.0 / math.sqrt(cells * space * time)
     vmem = pl.BlockSpec(memory_space=pltpu.VMEM)
+    hbm = pl.BlockSpec(memory_space=pltpu.HBM)
     dma = pltpu.SemaphoreType.DMA
     bf16 = jnp.bfloat16
     input_grad, weight_grad = pl.pallas_call(
@@ -462,9 +479,11 @@
             jax.ShapeDtypeStruct((cells, cin), bf16),
             jax.ShapeDtypeStruct((27, in_share, out_share), jnp.float32),
         ),
-        in_specs=[vmem, vmem, pl.BlockSpec(memory_space=pl.ANY)],
+        in_specs=[hbm, hbm, hbm],
         out_specs=(vmem, vmem),
         scratch_shapes=[
+            pltpu.VMEM((cells, cin), bf16),
+            pltpu.VMEM((cells, cout), bf16),
             pltpu.VMEM((27, cin, cout), bf16),
             pltpu.VMEM((3, 2 * cells, cin), bf16),
             pltpu.VMEM((3, 2 * cells, cout), bf16),
@@ -477,17 +496,16 @@
             pltpu.VMEM((space, time, frames * in_share, LANES), bf16),
             pltpu.VMEM((frames * out_share, (time + 1) * lanes), bf16),
             pltpu.VMEM((9, frames * in_share, time * lanes), bf16),
-            dma,
+            dma((3,)),
             dma((5,)), dma((5,)), dma((5,)), dma((5,)),
             dma((time - 1,)), dma((time - 1,)),
             dma((space - 1,)), dma((space - 1,)), dma((space - 1,)), dma((space - 1,)),
-            dma((space - 1,)), dma((space - 1,)), dma((time - 1,)), dma((time - 1,)),
+            dma((space - 1,)), dma((space - 1,)), dma((space * (time - 1),)), dma((space * (time - 1),)),
         ],
         compiler_params=pltpu.CompilerParams(
-            collective_id=0, has_side_effects=True, vmem_limit_bytes=62 * 1024 * 1024
+            collective_id=0, has_side_effects=True, vmem_limit_bytes=52 * 1024 * 1024
         ),
     )(inputs.reshape(cells, cin), cotangent.reshape(cells, cout), weight.reshape(27, cin, cout))
-    anywhere = pl.BlockSpec(memory_space=pl.ANY)
     input_grad, weight_grad = pl.pallas_call(
         written,
         out_shape=(
@@ -495,8 +513,9 @@
             jax.ShapeDtypeStruct(weight_grad.shape, jnp.float32),
         ),
         in_specs=[vmem, vmem],
-        out_specs=(anywhere, anywhere),
+        out_specs=(hbm, hbm),
         scratch_shapes=[dma((2,))],
+        compiler_params=pltpu.CompilerParams(vmem_limit_bytes=8 * 1024 * 1024),
     )(input_grad, weight_grad)
     return (
         input_grad.reshape(inputs.shape),

time: 33.9 us -> 33.4 us (0.985)
  the two profiles are of different devices: /device:TPU:1 before, /device:TPU:0 now
where the time goes in v3:
time: 33.4 us; the launch traced here: 33.2 us
  Pallas kernels  30.8 us (92%)
  local copies, waits for them, and re-layouts  1.78 us (5%)
  between operations  0.65 us (2%)
    pallas_call x1, Pallas kernels, gathered(): pl.pallas_call(functools.partial(kernel, space, time, width, factor), out...  29.9 us
    unnamed x4, local copies, waits for them, and re-layouts  1.78 us
    pallas_call x1, Pallas kernels, gathered(): pl.pallas_call(written, out_shape=(jax.ShapeDtypeStruct(input_grad.shape,...  0.88 us

profile of v3, /device:TPU:0, one launch (start us, length us, event | category | flops | bytes accessed | tf_op | source)
XLA Modules:
  0.0 33.2 jit_solution(14224818600670193454)
XLA Ops:
  0.6 0.0 copy-start
  0.6 0.9 %copy-done = bf16[2,1,96,192]{3,2,1,0:T(8,128)(2,1)S(1)} copy-done((bf16[2,1,96,192]{3,2,1,0:T(8,128)(2,1)S(1)}, bf16[2,1,96,192]{3,2,1,0:T(8,128)(2,1)}, u32[]{:S(2)}) %copy-start) | copy-done | bytes 73752
  1.5 0.0 copy-start.1
  1.5 0.9 %copy-done.1 = bf16[2,1,96,192]{3,2,1,0:T(8,128)(2,1)S(1)} copy-done((bf16[2,1,96,192]{3,2,1,0:T(8,128)(2,1)S(1)}, bf16[2,1,96,192]{3,2,1,0:T(8,128)(2,1)}, u32[]{:S(2)}) %copy-start.1) | copy-done | bytes 73752
  2.4 29.9 %shard_map.50 = (bf16[192,192]{1,0:T(8,128)(2,1)S(1)}, f32[27,48,48]{2,1,0:T(8,128)S(1)}) custom-call(bf16[192,192]{1,0:T(8,128)(2,1)S(1)} %bitcast.7, bf16[192,192]{1,0:T(8,128)(2,1)S(1)} %bitcast.8, bf16[27,192,192]{2,1,0:T(8,128)(2,1)} %bitcast.9), custom_call_target="tpu_custom_call" | custom-call | tf_op jit(solution)/shard_map/pallas_call | solution.py:476
  32.3 0.9 %shard_map.51 = (bf16[192,192]{1,0:T(8,128)(2,1)}, f32[27,48,48]{2,1,0:T(8,128)}) custom-call(bf16[192,192]{1,0:T(8,128)(2,1)S(1)} %get-tuple-element.6.ig_ref, f32[27,48,48]{2,1,0:T(8,128)S(1)} %get-tuple-element.7.wg_ref), custom_call_target="tpu_custom_call" | custom-call | tf_op jit(solution)/shard_map/pallas_call | solution.py:509
Async XLA Ops:
  0.6 0.9 %copy-start = (bf16[2,1,96,192]{3,2,1,0:T(8,128)(2,1)S(1)}, bf16[2,1,96,192]{3,2,1,0:T(8,128)(2,1)}, u32[]{:S(2)}) copy-start(bf16[2,1,96,192]{3,2,1,0:T(8,128)(2,1)} %param.3) | copy-start | bytes 221188
  1.5 0.9 %copy-start.1 = (bf16[2,1,96,192]{3,2,1,0:T(8,128)(2,1)S(1)}, bf16[2,1,96,192]{3,2,1,0:T(8,128)(2,1)}, u32[]{:S(2)}) copy-start(bf16[2,1,96,192]{3,2,1,0:T(8,128)(2,1)} %param.4) | copy-start | bytes 221188

commit v4 on v3

--- a/solution.py
+++ b/solution.py
@@ -352,6 +352,10 @@
     taps(xbuf, 1, (2,), True, sums)
     unpacked(x_halo[0], xheld, 0, xbuf, 1)
     taps(xbuf, 1, (0, 1), True, sums)
+    for copy in x1:
+        copy.wait_recv()
+    for sent, _, _, copy in hops[0]:
+        start_if(sent, copy)
     unpacked(x_halo[1], xheld, 1, xbuf, 1)
     taps(xbuf, 0, (2,), True, sums)
     unpacked(x_halo[2], xheld, 2, xbuf, 1)
@@ -359,10 +363,6 @@
     unpacked(x_halo[3], xheld, 3, xbuf, 1)
     taps(xbuf, 0, (0, 1), True, sums)
     unpacked(x_halo[4], xheld, 4, xbuf, 1)
-    for copy in x1:
-        copy.wait_recv()
-    for sent, _, _, copy in hops[0]:
-        start_if(sent, copy)
     taps(xbuf, 2, (0, 1), True, sums)
     outputs = shifted_rows(sums[0], -1, width) + sums[1] + shifted_rows(sums[2], 1, width)
     logistic = jax.nn.sigmoid(outputs)
@@ -380,14 +380,14 @@
     urecv[:, pl.ds(pl.multiple_of(t * lanes + z * LANES, LANES), LANES)] = uts[z]
     for copy in first[0]:
         copy.start()
+    hop_received(0)
+    if space > 2:
+        for sent, _, _, copy in hops[1]:
+            start_if(sent, copy)
     u_halo = halos(upack, uheld, hu_send, hu_recv, -1, early, late)
     for sent, _, _, _, copy in u_halo:
         start_if(sent, copy)
     ubuf[1, :cells] = upstream
-    hop_received(0)
-    if space > 2:
-        for sent, _, _, copy in hops[1]:
-            start_if(sent, copy)
     placed(z)
     sums = [None, None, None]
     taps(ubuf, 1, (2,), False, sums)

time: 33.4 us -> 30.8 us (0.922)
  the two profiles are of different devices: /device:TPU:0 before, /device:TPU:2 now
where the time goes in v4:
time: 30.8 us; the launch traced here: 30.6 us
  Pallas kernels  28.2 us (92%)
  local copies, waits for them, and re-layouts  1.78 us (6%)
  between operations  0.65 us (2%)
    pallas_call x1, Pallas kernels, gathered(): pl.pallas_call(functools.partial(kernel, space, time, width, factor), out...  27.3 us
    unnamed x4, local copies, waits for them, and re-layouts  1.78 us
    pallas_call x1, Pallas kernels, gathered(): pl.pallas_call(written, out_shape=(jax.ShapeDtypeStruct(input_grad.shape,...  0.88 us

profile of v4, /device:TPU:2, one launch (start us, length us, event | category | flops | bytes accessed | tf_op | source)
XLA Modules:
  0.0 30.6 jit_solution(9599474298511102498)
XLA Ops:
  0.6 0.0 copy-start
  0.6 0.9 %copy-done = bf16[2,1,96,192]{3,2,1,0:T(8,128)(2,1)S(1)} copy-done((bf16[2,1,96,192]{3,2,1,0:T(8,128)(2,1)S(1)}, bf16[2,1,96,192]{3,2,1,0:T(8,128)(2,1)}, u32[]{:S(2)}) %copy-start) | copy-done | bytes 73752
  1.5 0.0 copy-start.1
  1.5 0.9 %copy-done.1 = bf16[2,1,96,192]{3,2,1,0:T(8,128)(2,1)S(1)} copy-done((bf16[2,1,96,192]{3,2,1,0:T(8,128)(2,1)S(1)}, bf16[2,1,96,192]{3,2,1,0:T(8,128)(2,1)}, u32[]{:S(2)}) %copy-start.1) | copy-done | bytes 73752
  2.4 27.3 %shard_map.50 = (bf16[192,192]{1,0:T(8,128)(2,1)S(1)}, f32[27,48,48]{2,1,0:T(8,128)S(1)}) custom-call(bf16[192,192]{1,0:T(8,128)(2,1)S(1)} %bitcast.7, bf16[192,192]{1,0:T(8,128)(2,1)S(1)} %bitcast.8, bf16[27,192,192]{2,1,0:T(8,128)(2,1)} %bitcast.9), custom_call_target="tpu_custom_call" | custom-call | tf_op jit(solution)/shard_map/pallas_call | solution.py:476
  29.7 0.9 %shard_map.51 = (bf16[192,192]{1,0:T(8,128)(2,1)}, f32[27,48,48]{2,1,0:T(8,128)}) custom-call(bf16[192,192]{1,0:T(8,128)(2,1)S(1)} %get-tuple-element.6.ig_ref, f32[27,48,48]{2,1,0:T(8,128)S(1)} %get-tuple-element.7.wg_ref), custom_call_target="tpu_custom_call" | custom-call | tf_op jit(solution)/shard_map/pallas_call | solution.py:509
Async XLA Ops:
  0.6 0.9 %copy-start = (bf16[2,1,96,192]{3,2,1,0:T(8,128)(2,1)S(1)}, bf16[2,1,96,192]{3,2,1,0:T(8,128)(2,1)}, u32[]{:S(2)}) copy-start(bf16[2,1,96,192]{3,2,1,0:T(8,128)(2,1)} %param.3) | copy-start | bytes 221188
  1.5 0.9 %copy-start.1 = (bf16[2,1,96,192]{3,2,1,0:T(8,128)(2,1)S(1)}, bf16[2,1,96,192]{3,2,1,0:T(8,128)(2,1)}, u32[]{:S(2)}) copy-start(bf16[2,1,96,192]{3,2,1,0:T(8,128)(2,1)} %param.4) | copy-start | bytes 221188

commit v5 on v4

--- a/solution.py
+++ b/solution.py
@@ -273,12 +273,15 @@
 
     hops = []
     for step in range(space - 1):
-        up, down = xrecv.at[z - step], xrecv.at[z + step]
+        if step < 2:
+            up, down, far, has_up, has_down = xrecv.at[z - step], xrecv.at[z + step], 1, z >= step, z + step < space
+        else:
+            up, down, far, has_up, has_down = xrecv.at[z], xrecv.at[z], step + 1, above, below
         hops.append((
-            (above & (z >= step), below & (z > step), z - 1 - step,
-             remote(up, up, up_send, up_recv, step, at(1, 0))),
-            (below & (z + step < space), above & (z + step + 1 < space), z + 1 + step,
-             remote(down, down, down_send, down_recv, step, at(-1, 0))),
+            (has_up & (z + far < space), below & (z > step), z - 1 - step,
+             remote(up, up, up_send, up_recv, step, at(far, 0))),
+            (has_down & (z >= far), above & (z + step + 1 < space), z + 1 + step,
+             remote(down, down, down_send, down_recv, step, at(-far, 0))),
         ))
 
     couples = time // 2
@@ -387,6 +390,9 @@
     u_halo = halos(upack, uheld, hu_send, hu_recv, -1, early, late)
     for sent, _, _, _, copy in u_halo:
         start_if(sent, copy)
+    for hop in hops[2:]:
+        for sent, _, _, copy in hop:
+            start_if(sent, copy)
     ubuf[1, :cells] = upstream
     placed(z)
     sums = [None, None, None]
@@ -397,11 +403,6 @@
         for copy in first[step]:
             copy.start()
     hop_placed(0)
-    for step in range(1, space - 1):
-        hop_received(step)
-        if step + 1 < space - 1:
-            for sent, _, _, copy in hops[step + 1]:
-                start_if(sent, copy)
     handed_on(0)
     unpacked(u_halo[0], uheld, 0, ubuf, 0)
     taps(ubuf, 1, (0, 1), False, sums)
@@ -419,6 +420,7 @@
     total = shifted_rows(sums[0], 1, width) + sums[1] + shifted_rows(sums[2], -1, width)
     ig_ref[...] = total.astype(jnp.bfloat16)
     for step in range(1, space - 1):
+        hop_received(step)
         hop_placed(step)
 
     for piece in range(space):

time: 30.8 us -> 31 us (level)
  the two profiles are of different devices: /device:TPU:2 before, /device:TPU:1 now
where the time goes in v5:
time: 31 us; the launch traced here: 30.9 us
  Pallas kernels  28.4 us (92%)
  local copies, waits for them, and re-layouts  1.78 us (6%)
  between operations  0.65 us (2%)
    pallas_call x1, Pallas kernels, gathered(): pl.pallas_call(functools.partial(kernel, space, time, width, factor), out...  27.6 us
    unnamed x4, local copies, waits for them, and re-layouts  1.78 us
    pallas_call x1, Pallas kernels, gathered(): pl.pallas_call(written, out_shape=(jax.ShapeDtypeStruct(input_grad.shape,...  0.88 us

profile of v5, /device:TPU:1, one launch (start us, length us, event | category | flops | bytes accessed | tf_op | source)
XLA Modules:
  0.0 30.9 jit_solution(13348523554236438749)
XLA Ops:
  0.6 0.0 copy-start
  0.6 0.9 %copy-done = bf16[2,1,96,192]{3,2,1,0:T(8,128)(2,1)S(1)} copy-done((bf16[2,1,96,192]{3,2,1,0:T(8,128)(2,1)S(1)}, bf16[2,1,96,192]{3,2,1,0:T(8,128)(2,1)}, u32[]{:S(2)}) %copy-start) | copy-done | bytes 73752
  1.5 0.0 copy-start.1
  1.5 0.9 %copy-done.1 = bf16[2,1,96,192]{3,2,1,0:T(8,128)(2,1)S(1)} copy-done((bf16[2,1,96,192]{3,2,1,0:T(8,128)(2,1)S(1)}, bf16[2,1,96,192]{3,2,1,0:T(8,128)(2,1)}, u32[]{:S(2)}) %copy-start.1) | copy-done | bytes 73752
  2.4 27.6 %shard_map.50 = (bf16[192,192]{1,0:T(8,128)(2,1)S(1)}, f32[27,48,48]{2,1,0:T(8,128)S(1)}) custom-call(bf16[192,192]{1,0:T(8,128)(2,1)S(1)} %bitcast.7, bf16[192,192]{1,0:T(8,128)(2,1)S(1)} %bitcast.8, bf16[27,192,192]{2,1,0:T(8,128)(2,1)} %bitcast.9), custom_call_target="tpu_custom_call" | custom-call | tf_op jit(solution)/shard_map/pallas_call | solution.py:478
  30.0 0.9 %shard_map.51 = (bf16[192,192]{1,0:T(8,128)(2,1)}, f32[27,48,48]{2,1,0:T(8,128)}) custom-call(bf16[192,192]{1,0:T(8,128)(2,1)S(1)} %get-tuple-element.6.ig_ref, f32[27,48,48]{2,1,0:T(8,128)S(1)} %get-tuple-element.7.wg_ref), custom_call_target="tpu_custom_call" | custom-call | tf_op jit(solution)/shard_map/pallas_call | solution.py:511
Async XLA Ops:
  0.6 0.9 %copy-start = (bf16[2,1,96,192]{3,2,1,0:T(8,128)(2,1)S(1)}, bf16[2,1,96,192]{3,2,1,0:T(8,128)(2,1)}, u32[]{:S(2)}) copy-start(bf16[2,1,96,192]{3,2,1,0:T(8,128)(2,1)} %param.3) | copy-start | bytes 221188
  1.5 0.9 %copy-start.1 = (bf16[2,1,96,192]{3,2,1,0:T(8,128)(2,1)S(1)}, bf16[2,1,96,192]{3,2,1,0:T(8,128)(2,1)}, u32[]{:S(2)}) copy-start(bf16[2,1,96,192]{3,2,1,0:T(8,128)(2,1)} %param.4) | copy-start | bytes 221188
